TPU v7x, 128 devices: a whole 4x4x4 slice. The times are simulated.
128 devices in a mesh: segment: 4 (over y_lo, core), slab: 32 (over z, x, y_hi).
Axes of the slice: x: 4, y: 4 (y_hi: 2, y_lo: 2; y = y_hi * 2 + y_lo), z: 4, core: 2. Of those that a mesh axis runs over, the one named last changes fastest.
Arguments:
- video_in: bfloat16 [8, 64, 64, 384], P(None, 'slab'), may hold values from -6 to 6
- cache_in: bfloat16 [4, 2, 64, 64, 384], P('segment', None, 'slab'), may hold values from -0.25 to 2
- conv_weight: bfloat16 [4, 3, 3, 3, 384, 384], P('segment'), may hold values from -0.0625 to 0.0625
- conv_bias: float32 [4, 384], P('segment'), may hold values from -1.5 to 1.5
- norm_gain: float32 [4, 384], P('segment'), may hold values from 0.5 to 2
Outputs:
- video_out: bfloat16 [8, 64, 64, 384], P('segment', 'slab')
- cache_out: bfloat16 [4, 2, 64, 64, 384], P('segment', None, 'slab')
All inputs are finite; a program needn't handle non-finite values.
Results may differ from a plain program's by a relative error of at most 0.0067.
Values may be sent and summed in bfloat16 or wider, within the bound.
A program may use at most 64 MiB of HBM per device.

v0:
```python
import jax
import jax.numpy as jnp
from jax import lax
from jax.experimental import pallas as pl
from jax.experimental.pallas import tpu as pltpu
from jax.sharding import PartitionSpec as P

MESH = pl.DeviceIdType.MESH
PAD = 8
ORDER = (1, 0, 2)


def kernel(video, cache, weight, bias, gain, vout, cout, wbuf, xin, cin, lhs, flat, acc, outb, actb,
           w_sem, loc_sem, in_sem, pipe_send, vin_send, cin_loc, cin_sem, cin_send, vo_send, vo_sem, co_sem):
    frames, held, columns, channels = video.shape
    pitch = columns + PAD
    size = held * columns
    block = 3 * channels
    seg = lax.axis_index("segment")
    slab = lax.axis_index("slab")
    last = lax.axis_size("segment") - 1
    per = frames // (last + 1)
    has_up = jnp.logical_not(slab == 0)
    has_down = jnp.logical_not(slab == lax.axis_size("slab") - 1)
    other = (last - seg, slab)
    first_seg = seg == 0
    above = lax.rem(slab + lax.axis_size("slab") - 1, lax.axis_size("slab"))
    below = lax.rem(slab + 1, lax.axis_size("slab"))
    before = lax.rem(seg + last, last + 1)
    after = lax.rem(seg + 1, last + 1)

    def remote(src, dst, send, recv, dev):
        return pltpu.make_async_remote_copy(src_ref=src, dst_ref=dst, send_sem=send, recv_sem=recv, device_id=dev, device_id_type=MESH)

    def w_copy(a, b):
        return pltpu.make_async_copy(
            weight.at[a, pl.ds(b * block, block), :],
            wbuf.at[pl.ds(ORDER.index(b) * block, block), pl.ds((2 - a) * channels, channels)],
            w_sem.at[a, b])

    def own_video(f):
        return pltpu.make_async_copy(video.at[f], xin.at[f, pl.ds(1, held)], loc_sem.at[f])

    own_cache = pltpu.make_async_copy(cache, cin.at[:, pl.ds(1, held)], cin_loc)

    @pl.when(first_seg)
    def _():
        own_video(0).start()

    w_copy(2, 1).start()
    w_copy(2, 0).start()
    w_copy(2, 2).start()
    own_cache.start()

    @pl.when(first_seg)
    def _():
        for f in range(1, frames):
            own_video(f).start()

    for a in (1, 0):
        for b in ORDER:
            w_copy(a, b).start()

    barrier = pltpu.get_barrier_semaphore()

    def greet(s, q):
        pl.semaphore_signal(barrier, inc=1, device_id=(s, q), device_id_type=MESH)

    later_seg = seg > 0
    early_seg = seg < last
    pl.when(has_up)(lambda: greet(seg, above))
    pl.when(has_down)(lambda: greet(seg, below))

    @pl.when(later_seg)
    def _():
        greet(before, slab)
        pl.when(has_up)(lambda: greet(before, above))
        pl.when(has_down)(lambda: greet(before, below))

    @pl.when(first_seg)
    def _():
        pl.when(has_up)(lambda: greet(2, above))
        pl.when(has_down)(lambda: greet(3, below))

    @pl.when(early_seg)
    def _():
        greet(last, slab)

    flat[...] = jnp.zeros_like(flat)
    acc[...] = jnp.zeros_like(acc)

    @pl.when(jnp.logical_not(has_up))
    def _():
        xin[:, 0] = jnp.zeros_like(xin[:, 0])
        cin[:, 0] = jnp.zeros_like(cin[:, 0])

    @pl.when(jnp.logical_not(has_down))
    def _():
        xin[:, held + 1] = jnp.zeros_like(xin[:, held + 1])
        cin[:, held + 1] = jnp.zeros_like(cin[:, held + 1])

    one = jnp.int32(1)
    zero = jnp.int32(0)
    ups = jnp.where(has_up, one, zero)
    downs = jnp.where(has_down, one, zero)
    expected = ups + downs
    expected += jnp.where(early_seg, 1 + ups + downs, zero)
    expected += jnp.where(seg == 2, downs, zero)
    expected += jnp.where(seg == last, ups + last, zero)
    pl.semaphore_wait(barrier, expected)

    sends_down = jnp.logical_and(seg == 2, has_down)
    sends_up = jnp.logical_and(seg == 3, has_up)

    def vin_down(f):
        return remote(video.at[f, held - 1], xin.at[f, 0], vin_send.at[f], in_sem.at[f, 1], (0, below))

    def vin_up(f):
        return remote(video.at[f, 0], xin.at[f, held + 1], vin_send.at[f], in_sem.at[f, 2], (0, above))

    def cache_down():
        return remote(cache.at[:, held - 1], cin.at[:, 0], cin_send.at[0], cin_sem.at[0], (seg, below))

    def cache_up():
        return remote(cache.at[:, 0], cin.at[:, held + 1], cin_send.at[1], cin_sem.at[1], (seg, above))

    @pl.when(sends_down)
    def _():
        for f in range(frames):
            vin_down(f).start()

    @pl.when(sends_up)
    def _():
        for f in range(frames):
            vin_up(f).start()

    def send_cache():
        pl.when(has_down)(lambda: cache_down().start())
        pl.when(has_up)(lambda: cache_up().start())

    pl.when(first_seg)(send_cache)

    gains = gain[0:1, :]
    biases = bias[0:1, :]

    def put(r, values):
        flat[r * pitch + PAD:(r + 1) * pitch] = values

    def copy_taps(b, r):
        for c in range(3):
            start = (r + b) * pitch + PAD + c - 1
            at = ORDER.index(b) * block + c * channels
            lhs[r * columns:(r + 1) * columns, at:at + channels] = flat[start:start + columns].astype(jnp.bfloat16)

    inner_taps = [(b, r) for b in ORDER for r in range(held) if 1 <= r + b <= held]
    outer_taps = [(b, r) for b in ORDER for r in range(held) if not 1 <= r + b <= held]

    def activate(values):
        values = values.astype(jnp.float32)
        mean = jnp.sum(values * values, axis=-1, keepdims=True) * (1.0 / channels)
        scaled = values * lax.rsqrt(mean + 1e-06) * gains
        return scaled / (1.0 + jnp.exp(-scaled))

    def cached_frames():
        own_cache.wait()
        pl.when(has_up)(lambda: remote(cache.at[:, 0], cin.at[:, 0], cin_send.at[0], cin_sem.at[0], other).wait_recv())
        pl.when(has_down)(lambda: remote(cache.at[:, 0], cin.at[:, held + 1], cin_send.at[1], cin_sem.at[1], other).wait_recv())

        def load(j):
            for r in range(held + 2):
                put(r, cin[j, r].astype(jnp.float32))
            for b, r in inner_taps + outer_taps:
                copy_taps(b, r)

        load(1)
        later = jnp.dot(lhs[...], wbuf[:, channels:], preferred_element_type=jnp.float32)
        acc[0] += later[:, :channels]
        acc[1] += later[:, channels:]
        load(0)
        acc[0] += jnp.dot(lhs[...], wbuf[:, 2 * channels:], preferred_element_type=jnp.float32)

    def wait_weights(a):
        for b in ORDER:
            w_copy(a, b).wait()

    @pl.when(later_seg)
    def _():
        wait_weights(2)
        wait_weights(1)
        wait_weights(0)
        send_cache()
        cached_frames()

    def pipe_own(f):
        return remote(outb.at[f], xin.at[f, pl.ds(1, held)], pipe_send.at[f, 0], in_sem.at[f, 0], (after, slab))

    def pipe_up(f):
        return remote(outb.at[f, 0], xin.at[f, held + 1], pipe_send.at[f, 1], in_sem.at[f, 2], (after, above))

    def pipe_down(f):
        return remote(outb.at[f, held - 1], xin.at[f, 0], pipe_send.at[f, 2], in_sem.at[f, 1], (after, below))

    def vo_copy(f):
        return remote(outb.at[f], vout.at[f % per], vo_send.at[f], vo_sem.at[f % per], (f // per, slab))

    def vo_local(f):
        return pltpu.make_async_copy(outb.at[f], vout.at[f % per], vo_sem.at[f % per])

    def co_local(j):
        return pltpu.make_async_copy(actb.at[j], cout.at[j], co_sem.at[j])

    def frame(f, carry):
        now = lax.rem(f, 3)

        @pl.when(first_seg)
        def _():
            own_video(f).wait()

        @pl.when(later_seg)
        def _():
            remote(outb.at[f], xin.at[f, pl.ds(1, held)], vin_send.at[f], in_sem.at[f, 0], other).wait_recv()

        for r in range(1, 1 + held):
            acts = activate(xin[f, r])
            put(r, acts)

        for b, r in inner_taps:
            copy_taps(b, r)

        @pl.when(f >= frames - 2)
        def _():
            j = f - (frames - 2)
            for r in range(held):
                actb[j, r] = flat[(r + 1) * pitch + PAD:(r + 2) * pitch].astype(jnp.bfloat16)
            co_local(j).start()

        @pl.when(jnp.logical_and(first_seg, f == 0))
        def _():
            wait_weights(2)

        acc[now] += jnp.dot(lhs[:, :block], wbuf[:block, :channels], preferred_element_type=jnp.float32)

        pl.when(has_up)(lambda: remote(outb.at[f, 0], xin.at[f, 0], vin_send.at[f], in_sem.at[f, 1], other).wait_recv())
        pl.when(has_down)(lambda: remote(outb.at[f, 0], xin.at[f, held + 1], vin_send.at[f], in_sem.at[f, 2], other).wait_recv())

        for r in (0, held + 1):
            put(r, activate(xin[f, r]))
        for b, r in outer_taps:
            copy_taps(b, r)

        conv = jnp.dot(lhs[:, block:], wbuf[block:, :channels], preferred_element_type=jnp.float32) + acc[now] + biases

        @pl.when(jnp.logical_and(first_seg, f == 0))
        def _():
            wait_weights(1)
            wait_weights(0)
            acc[0] = conv
            cached_keep = lhs[...]
            cached_frames()
            lhs[...] = cached_keep
            outb[f] = (xin[f, 1:1 + held].astype(jnp.float32).reshape(size, channels) + acc[0]).reshape(held, columns, channels).astype(jnp.bfloat16)

        @pl.when(jnp.logical_not(jnp.logical_and(first_seg, f == 0)))
        def _():
            outb[f] = (xin[f, 1:1 + held].astype(jnp.float32).reshape(size, channels) + conv).reshape(held, columns, channels).astype(jnp.bfloat16)

        @pl.when(early_seg)
        def _():
            pl.when(has_up)(lambda: pipe_up(f).start())
            pl.when(has_down)(lambda: pipe_down(f).start())
            pipe_own(f).start()

        @pl.when(seg == last)
        def _():
            pl.when(f // per < last)(lambda: vo_copy(f).start())
            pl.when(f // per == last)(lambda: vo_local(f).start())

        @pl.when(f < frames - 1)
        def _():
            later = jnp.dot(lhs[...], wbuf[:, channels:], preferred_element_type=jnp.float32)
            acc[lax.rem(f + 1, 3)] += later[:, :channels]
            acc[lax.rem(f + 2, 3)] = later[:, channels:]

        return carry

    lax.fori_loop(0, frames, frame, 0)

    for j in range(2):
        co_local(j).wait()

    @pl.when(early_seg)
    def _():
        for j in range(per):
            remote(outb.at[0], vout.at[j], vo_send.at[0], vo_sem.at[j], other).wait_recv()

        def sent(f, carry):
            pipe_own(f).wait_send()
            pl.when(has_up)(lambda: pipe_up(f).wait_send())
            pl.when(has_down)(lambda: pipe_down(f).wait_send())
            return carry

        lax.fori_loop(0, frames, sent, 0)

    @pl.when(seg == last)
    def _():
        for f in range(frames):
            if f // per < last:
                vo_copy(f).wait_send()
            else:
                vo_local(f).wait()

    pl.when(has_down)(lambda: cache_down().wait_send())
    pl.when(has_up)(lambda: cache_up().wait_send())

    @pl.when(sends_down)
    def _():
        for f in range(frames):
            vin_down(f).wait_send()

    @pl.when(sends_up)
    def _():
        for f in range(frames):
            vin_up(f).wait_send()


def local(video_in, cache_in, conv_weight, conv_bias, norm_gain):
    frames, held, columns, channels = video_in.shape
    rows = held + 2
    size = held * columns
    weight = conv_weight.reshape(3, 9 * channels, channels)
    cache = cache_in[0]
    per = frames // lax.axis_size("segment")
    dma = pltpu.SemaphoreType.DMA
    video_out, cache_out = pl.pallas_call(
        kernel,
        out_shape=(
            jax.ShapeDtypeStruct((per, held, columns, channels), jnp.bfloat16),
            jax.ShapeDtypeStruct(cache.shape, jnp.bfloat16),
        ),
        in_specs=[pl.BlockSpec(memory_space=pl.ANY)] * 3 + [pl.BlockSpec(memory_space=pltpu.VMEM)] * 2,
        out_specs=(pl.BlockSpec(memory_space=pl.ANY), pl.BlockSpec(memory_space=pl.ANY)),
        scratch_shapes=[
            pltpu.VMEM((9 * channels, 3 * channels), jnp.bfloat16),
            pltpu.VMEM((frames, rows, columns, channels), jnp.bfloat16),
            pltpu.VMEM((2, rows, columns, channels), jnp.bfloat16),
            pltpu.VMEM((size, 9 * channels), jnp.bfloat16),
            pltpu.VMEM((rows * (columns + PAD) + 8 * PAD, channels), jnp.float32),
            pltpu.VMEM((3, size, channels), jnp.float32),
            pltpu.VMEM((frames, held, columns, channels), jnp.bfloat16),
            pltpu.VMEM((2, held, columns, channels), jnp.bfloat16),
            dma((3, 3)), dma((frames,)), dma((frames, 3)), dma((frames, 3)), dma((frames,)),
            dma, dma((2,)), dma((2,)), dma((frames,)), dma((per,)), dma((2,)),
        ],
        compiler_params=pltpu.CompilerParams(collective_id=0, has_side_effects=True, vmem_limit_bytes=60 * 2**20),
    )(video_in, cache, weight, conv_bias, norm_gain)
    return video_out, cache_out[None]


def solution(mesh):
    return jax.shard_map(
        local,
        mesh=mesh,
        in_specs=(
            P(None, "slab", None, None),
            P("segment", None, "slab", None, None),
            P("segment", None, None, None, None, None),
            P("segment", None),
            P("segment", None),
        ),
        out_specs=(P("segment", "slab", None, None), P("segment", None, "slab", None, None)),
        check_vma=False,
    )
```

profile of v0, /device:TPU:105, one launch (start us, length us, event | category | flops | bytes accessed | tf_op | source)
XLA Modules:
  0.0 56.7 jit_solution(16426857390376443201)
XLA Ops:
  0.6 52.9 %shard_map.68 = (bf16[2,2,64,384]{3,2,1,0:T(8,128)(2,1)}, bf16[2,2,64,384]{3,2,1,0:T(8,128)(2,1)}) custom-call(bf16[8,2,64,384]{3,2,1,0:T(8,128)(2,1)} %video.1, bf16[2,2,64,384]{3,2,1,0:T(8,128)(2,1)} %bitcast.5, bf16[3,3456,384]{2,1,0:T(8,128)(2,1)} %bitcast.3, f32[1,384]{1,0:T(1,128)} %bias.1, f32[1,384]{1,0:T(1,128)} %gain.1), custom_call_target="tpu_custom_call" | custom-call | tf_op jit(solution)/shard_map/pallas_call | solution.py:334
  53.5 1.6 %copy.9 = bf16[2,2,64,384]{3,2,1,0:T(8,128)(2,1)} copy(bf16[2,2,64,384]{3,2,1,0:T(8,128)(2,1)} %get-tuple-element.8) | data formatting | bytes 393216
  55.1 1.6 %copy.10 = bf16[1,2,2,64,384]{4,3,2,1,0:T(8,128)(2,1)} copy(bf16[1,2,2,64,384]{4,3,2,1,0:T(8,128)(2,1)} %bitcast.4) | data formatting | bytes 393216
where the time goes:
time: 56.9 us; the launch traced here: 56.7 us
  Pallas kernels  52.9 us (93%)
  local copies, waits for them, and re-layouts  3.25 us (6%)
  between operations  0.64 us (1%)
    pallas_call x1, Pallas kernels, local(): pl.pallas_call(kernel, out_shape=(jax.ShapeDtypeStruct((per, held, column...  52.9 us
    unnamed x2, local copies, waits for them, and re-layouts  3.25 us

commit v1 on v0

--- a/solution.py
+++ b/solution.py
@@ -8,9 +8,10 @@
 MESH = pl.DeviceIdType.MESH
 PAD = 8
 ORDER = (1, 0, 2)
-
-
-def kernel(video, cache, weight, bias, gain, vout, cout, wbuf, xin, cin, lhs, flat, acc, outb, actb,
+EARLY = 2
+
+
+def kernel(video, cache, weight, bias, gain, out, wbuf, xin, cin, lhs, flat, acc, outb, actb,
            w_sem, loc_sem, in_sem, pipe_send, vin_send, cin_loc, cin_sem, cin_send, vo_send, vo_sem, co_sem):
     frames, held, columns, channels = video.shape
     pitch = columns + PAD
@@ -24,6 +25,8 @@
     has_down = jnp.logical_not(slab == lax.axis_size("slab") - 1)
     other = (last - seg, slab)
     first_seg = seg == 0
+    vout = out.at[0]
+    cout = out.at[1]
     above = lax.rem(slab + lax.axis_size("slab") - 1, lax.axis_size("slab"))
     below = lax.rem(slab + 1, lax.axis_size("slab"))
     before = lax.rem(seg + last, last + 1)
@@ -126,12 +129,12 @@
 
     @pl.when(sends_down)
     def _():
-        for f in range(frames):
+        for f in range(EARLY):
             vin_down(f).start()
 
     @pl.when(sends_up)
     def _():
-        for f in range(frames):
+        for f in range(EARLY):
             vin_up(f).start()
 
     def send_cache():
@@ -139,6 +142,17 @@
         pl.when(has_up)(lambda: cache_up().start())
 
     pl.when(first_seg)(send_cache)
+
+    def send_edges(start, stop):
+        @pl.when(sends_down)
+        def _():
+            for f in range(start, stop):
+                vin_down(f).start()
+
+        @pl.when(sends_up)
+        def _():
+            for f in range(start, stop):
+                vin_up(f).start()
 
     gains = gain[0:1, :]
     biases = bias[0:1, :]
@@ -188,8 +202,10 @@
         wait_weights(2)
         wait_weights(1)
         wait_weights(0)
+        send_edges(EARLY, 2 * EARLY)
         send_cache()
         cached_frames()
+        send_edges(2 * EARLY, frames)
 
     def pipe_own(f):
         return remote(outb.at[f], xin.at[f, pl.ds(1, held)], pipe_send.at[f, 0], in_sem.at[f, 0], (after, slab))
@@ -331,14 +347,11 @@
     cache = cache_in[0]
     per = frames // lax.axis_size("segment")
     dma = pltpu.SemaphoreType.DMA
-    video_out, cache_out = pl.pallas_call(
+    both = pl.pallas_call(
         kernel,
-        out_shape=(
-            jax.ShapeDtypeStruct((per, held, columns, channels), jnp.bfloat16),
-            jax.ShapeDtypeStruct(cache.shape, jnp.bfloat16),
-        ),
+        out_shape=jax.ShapeDtypeStruct((2, per, held, columns, channels), jnp.bfloat16),
         in_specs=[pl.BlockSpec(memory_space=pl.ANY)] * 3 + [pl.BlockSpec(memory_space=pltpu.VMEM)] * 2,
-        out_specs=(pl.BlockSpec(memory_space=pl.ANY), pl.BlockSpec(memory_space=pl.ANY)),
+        out_specs=pl.BlockSpec(memory_space=pl.ANY),
         scratch_shapes=[
             pltpu.VMEM((9 * channels, 3 * channels), jnp.bfloat16),
             pltpu.VMEM((frames, rows, columns, channels), jnp.bfloat16),
@@ -353,7 +366,7 @@
         ],
         compiler_params=pltpu.CompilerParams(collective_id=0, has_side_effects=True, vmem_limit_bytes=60 * 2**20),
     )(video_in, cache, weight, conv_bias, norm_gain)
-    return video_out, cache_out[None]
+    return both[0], both[1][None]
 
 
 def solution(mesh):

time: 56.9 us -> 53.8 us (0.946)
  Pallas kernels: 52.9 us -> 50.9 us
  local copies, waits for them, and re-layouts: 3.25 us -> 1.8 us
    unnamed x2 -> x0, local copies, waits for them, and re-layouts: 3.25 us -> none
    pallas_call x1, Pallas kernels: 52.9 us -> 50.9 us  [local(): pl.pallas_call(kernel, out_shape=jax.ShapeDtypeStruct((2, per, held, colu...]
    slice x0 -> x1, local copies, waits for them, and re-layouts: none -> 1.8 us  [local(): return (both[0], both[1][None])]
where the time goes in v1:
time: 53.8 us; the launch traced here: 53.3 us
  Pallas kernels  50.9 us (95%)
  local copies, waits for them, and re-layouts  1.8 us (3%)
  between operations  0.64 us (1%)
    pallas_call x1, Pallas kernels, local(): pl.pallas_call(kernel, out_shape=jax.ShapeDtypeStruct((2, per, held, colu...  50.9 us
    slice x1, local copies, waits for them, and re-layouts, local(): return (both[0], both[1][None])  1.8 us

profile of v1, /device:TPU:105, one launch (start us, length us, event | category | flops | bytes accessed | tf_op | source)
XLA Modules:
  0.0 53.3 jit_solution(15558004651012558416)
XLA Ops:
  0.6 50.9 %shard_map.68 = bf16[2,2,2,64,384]{4,3,2,1,0:T(8,128)(2,1)} custom-call(bf16[8,2,64,384]{3,2,1,0:T(8,128)(2,1)} %video.1, bf16[2,2,64,384]{3,2,1,0:T(8,128)(2,1)} %bitcast.5, bf16[3,3456,384]{2,1,0:T(8,128)(2,1)} %bitcast.4, f32[1,384]{1,0:T(1,128)} %bias.1, f32[1,384]{1,0:T(1,128)} %gain.1), custom_call_target="tpu_custom_call" | custom-call | tf_op jit(solution)/shard_map/pallas_call | solution.py:350
  51.5 1.8 %fusion = (bf16[1,2,2,64,384]{4,3,2,1,0:T(8,128)(2,1)}, bf16[2,2,64,384]{3,2,1,0:T(8,128)(2,1)}) fusion(bf16[2,2,2,64,384]{4,3,2,1,0:T(8,128)(2,1)} %shard_map.68), kind=kLoop, calls=%fused_computation.1 | loop fusion | bytes 786432 | tf_op jit(solution)/shard_map/slice | solution.py:369

commit v2 on v1

--- a/solution.py
+++ b/solution.py
@@ -202,8 +202,8 @@
         wait_weights(2)
         wait_weights(1)
         wait_weights(0)
+        send_cache()
         send_edges(EARLY, 2 * EARLY)
-        send_cache()
         cached_frames()
         send_edges(2 * EARLY, frames)
 
@@ -282,8 +282,16 @@
 
         @pl.when(early_seg)
         def _():
-            pl.when(has_up)(lambda: pipe_up(f).start())
-            pl.when(has_down)(lambda: pipe_down(f).start())
+            @pl.when(slab % 2 == 0)
+            def _():
+                pl.when(has_up)(lambda: pipe_up(f).start())
+                pipe_down(f).start()
+
+            @pl.when(slab % 2 == 1)
+            def _():
+                pl.when(has_down)(lambda: pipe_down(f).start())
+                pipe_up(f).start()
+
             pipe_own(f).start()
 
         @pl.when(seg == last)

time: 53.8 us -> 53.6 us (level)
  no operation moved by 1% of the time
where the time goes in v2:
time: 53.6 us; the launch traced here: 53.4 us
  Pallas kernels  51 us (95%)
  local copies, waits for them, and re-layouts  1.8 us (3%)
  between operations  0.64 us (1%)
    pallas_call x1, Pallas kernels, local(): pl.pallas_call(kernel, out_shape=jax.ShapeDtypeStruct((2, per, held, colu...  51 us
    slice x1, local copies, waits for them, and re-layouts, local(): return (both[0], both[1][None])  1.8 us

profile of v2, /device:TPU:105, one launch (start us, length us, event | category | flops | bytes accessed | tf_op | source)
XLA Modules:
  0.0 53.4 jit_solution(5734226323603571558)
XLA Ops:
  0.6 51.0 %shard_map.68 = bf16[2,2,2,64,384]{4,3,2,1,0:T(8,128)(2,1)} custom-call(bf16[8,2,64,384]{3,2,1,0:T(8,128)(2,1)} %video.1, bf16[2,2,64,384]{3,2,1,0:T(8,128)(2,1)} %bitcast.5, bf16[3,3456,384]{2,1,0:T(8,128)(2,1)} %bitcast.4, f32[1,384]{1,0:T(1,128)} %bias.1, f32[1,384]{1,0:T(1,128)} %gain.1), custom_call_target="tpu_custom_call" | custom-call | tf_op jit(solution)/shard_map/pallas_call | solution.py:358
  51.6 1.8 %fusion = (bf16[1,2,2,64,384]{4,3,2,1,0:T(8,128)(2,1)}, bf16[2,2,64,384]{3,2,1,0:T(8,128)(2,1)}) fusion(bf16[2,2,2,64,384]{4,3,2,1,0:T(8,128)(2,1)} %shard_map.68), kind=kLoop, calls=%fused_computation.1 | loop fusion | bytes 786432 | tf_op jit(solution)/shard_map/slice | solution.py:377

commit v3 on v2

--- a/solution.py
+++ b/solution.py
@@ -8,7 +8,7 @@
 MESH = pl.DeviceIdType.MESH
 PAD = 8
 ORDER = (1, 0, 2)
-EARLY = 2
+EARLY = 3
 
 
 def kernel(video, cache, weight, bias, gain, out, wbuf, xin, cin, lhs, flat, acc, outb, actb,
@@ -203,9 +203,9 @@
         wait_weights(1)
         wait_weights(0)
         send_cache()
-        send_edges(EARLY, 2 * EARLY)
+        send_edges(EARLY, EARLY + 2)
         cached_frames()
-        send_edges(2 * EARLY, frames)
+        send_edges(EARLY + 2, frames)
 
     def pipe_own(f):
         return remote(outb.at[f], xin.at[f, pl.ds(1, held)], pipe_send.at[f, 0], in_sem.at[f, 0], (after, slab))

time: 53.6 us -> 53.6 us (level)
  no operation moved by 1% of the time
where the time goes in v3:
time: 53.6 us; the launch traced here: 53.4 us
  Pallas kernels  51 us (95%)
  local copies, waits for them, and re-layouts  1.8 us (3%)
  between operations  0.64 us (1%)
    pallas_call x1, Pallas kernels, local(): pl.pallas_call(kernel, out_shape=jax.ShapeDtypeStruct((2, per, held, colu...  51 us
    slice x1, local copies, waits for them, and re-layouts, local(): return (both[0], both[1][None])  1.8 us

profile of v3, /device:TPU:105, one launch (start us, length us, event | category | flops | bytes accessed | tf_op | source)
XLA Modules:
  0.0 53.4 jit_solution(2280113113035769055)
XLA Ops:
  0.6 51.0 %shard_map.68 = bf16[2,2,2,64,384]{4,3,2,1,0:T(8,128)(2,1)} custom-call(bf16[8,2,64,384]{3,2,1,0:T(8,128)(2,1)} %video.1, bf16[2,2,64,384]{3,2,1,0:T(8,128)(2,1)} %bitcast.5, bf16[3,3456,384]{2,1,0:T(8,128)(2,1)} %bitcast.4, f32[1,384]{1,0:T(1,128)} %bias.1, f32[1,384]{1,0:T(1,128)} %gain.1), custom_call_target="tpu_custom_call" | custom-call | tf_op jit(solution)/shard_map/pallas_call | solution.py:358
  51.6 1.8 %fusion = (bf16[1,2,2,64,384]{4,3,2,1,0:T(8,128)(2,1)}, bf16[2,2,64,384]{3,2,1,0:T(8,128)(2,1)}) fusion(bf16[2,2,2,64,384]{4,3,2,1,0:T(8,128)(2,1)} %shard_map.68), kind=kLoop, calls=%fused_computation.1 | loop fusion | bytes 786432 | tf_op jit(solution)/shard_map/slice | solution.py:377
